TPU v7x, 32 devices: a whole 2x2x4 slice. The times are simulated.
32 devices in a mesh: band: 4 (over y, x), query: 8 (over z, core).
Axes of the slice: x: 2, y: 2, z: 4, core: 2. Of those that a mesh axis runs over, the one named last changes fastest.
Arguments:
- spectra: bfloat16 [192, 20480], P('band'), may hold values from 0 to 3
- theo: bfloat16 [8, 8, 20480], P('query', 'band'), may hold values from -0.0390625 to 0.0390625
- offsets: int32 [16], replicated, may hold values from -128 to 128
- win_lo: int32 [192], P('band'), may hold values from 0 to 32
- win_len: int32 [192], P('band'), may hold values from 1 to 32
Outputs:
- best: float32 [192, 16], P(('band', 'query'))
- average: float32 [192, 16], P(('band', 'query'))
Inputs may be any that keep to these rules, and one draw needn't show every extreme that they name: win_lo + win_len never exceeds 64.
All inputs are finite; a program needn't handle non-finite values.
Results may differ from a plain program's by a relative error of at most 0.003.
Values may be sent and summed in bfloat16 or wider, within the bound.
A program may use at most 128 MiB of HBM per device.

v0:
```python
import jax
import jax.numpy as jnp
from jax import lax
from jax.sharding import PartitionSpec as P

BG_HALF = 75
SHIFT_MAX = 128


def box_table():
    source = lax.broadcasted_iota(jnp.int32, (384, 128), 0)
    target = lax.broadcasted_iota(jnp.int32, (384, 128), 1)
    offset_gap = source - 128 - target
    inside = (jnp.abs(offset_gap) <= BG_HALF) & (offset_gap != 0)
    return inside.astype(jnp.bfloat16)


def correct(intensity):
    row_count, bin_count = intensity.shape
    block_count = bin_count // 128
    blocks = intensity.reshape(row_count, block_count, 128)
    zero_block = jnp.zeros((row_count, 1, 128), intensity.dtype)
    previous = jnp.concatenate([zero_block, blocks[:, :-1]], axis=1)
    following = jnp.concatenate([blocks[:, 1:], zero_block], axis=1)
    stacked = jnp.concatenate([previous, blocks, following], axis=2)
    window_sum = jnp.einsum("rbj,ji->rbi", stacked, box_table(), preferred_element_type=jnp.float32)
    result = blocks.astype(jnp.float32) - window_sum / (2.0 * BG_HALF)
    return result.astype(jnp.bfloat16).reshape(row_count, bin_count)


def shifted_copies(peptides, offsets):
    bin_count = peptides.shape[1]
    padded = jnp.pad(peptides, ((0, 0), (SHIFT_MAX, SHIFT_MAX)))

    def take_shift(offset):
        return lax.dynamic_slice_in_dim(padded, SHIFT_MAX - offset, bin_count, 1)

    copies = jax.vmap(take_shift, out_axes=1)(offsets)
    return copies.reshape(-1, bin_count)


def local(spectra, theo, offsets, win_lo, win_len):
    query_count = lax.axis_size("query")
    spectra_rows = spectra.shape[0]
    own_rows = spectra_rows // query_count
    own_start = lax.axis_index("query") * own_rows
    corrected = correct(spectra)
    shift_count = offsets.shape[0]
    group_size = theo.shape[1] * lax.axis_size("band")
    piece = lax.all_gather(theo, "band", axis=1, tiled=True)
    piece_rows = piece.shape[1]
    copies = shifted_copies(piece[0], offsets)
    partial_scores = jnp.einsum("mb,sb->ms", copies, corrected, preferred_element_type=jnp.float32)
    scores = partial_scores.reshape(1, piece_rows, shift_count * spectra_rows)
    score_table = scores.reshape(group_size, shift_count, query_count, own_rows)
    low_own = lax.dynamic_slice_in_dim(win_lo, own_start, own_rows, 0)
    length_own = lax.dynamic_slice_in_dim(win_len, own_start, own_rows, 0)
    gathered = lax.all_to_all(score_table, "query", split_axis=2, concat_axis=0, tiled=True)
    total_peptides = gathered.shape[0]
    owned_scores = gathered.reshape(total_peptides, shift_count, own_rows)
    peptide_index = lax.broadcasted_iota(jnp.int32, (total_peptides, own_rows), 0)
    inside = (peptide_index >= low_own[None, :]) & (peptide_index < (low_own + length_own)[None, :])
    best_score = jnp.max(jnp.where(inside[:, None, :], owned_scores, -jnp.inf), axis=0).T
    totals = jnp.sum(jnp.where(inside[:, None, :], owned_scores, 0.0), axis=0).T
    average = totals / length_own[:, None].astype(jnp.float32)
    return (best_score, average)


def solution(mesh):
    placed = (P("band", None), P("query", "band", None), P(), P("band"), P("band"))
    return jax.shard_map(
        local,
        mesh=mesh,
        in_specs=placed,
        out_specs=(P(("band", "query"), None), P(("band", "query"), None)),
        check_vma=False,
    )
```

profile of v0, /device:TPU:0, one launch (start us, length us, event | category | flops | bytes accessed | tf_op | source)
XLA Modules:
  0.0 84.9 jit_solution(6701654885838280901)
XLA Ops:
  0.7 1.2 %copy.17 = bf16[1,2,20480]{2,0,1:T(2,128)(2,1)S(1)} copy(bf16[1,2,20480]{2,1,0:T(2,128)(2,1)} %param.6) | data formatting | bytes 163840 | tf_op args[1]
  1.8 12.0 %all_gather.3 = bf16[1,8,20480]{2,0,1:T(2,128)(2,1)S(1)} all-gather(bf16[1,2,20480]{2,0,1:T(2,128)(2,1)S(1)} %copy.17), channel_id=1, replica_groups=mesh['band'=4,'query'=8] {'band'}, dimensions={1}, use_global_device_ids=true | all-gather | bytes 409600 | tf_op jit(solution)/shard_map/all_gather | solution.py:50
  13.8 0.4 copy.28
  14.2 0.7 fusion.29
  14.9 34.0 %while.1 = (s32[]{:T(128)}, bf16[8,20736]{1,0:T(8,128)(2,1)S(1)}, s32[16,2]{0,1:T(2,128)S(1)}, bf16[16,8,20480]{2,1,0:T(8,128)(2,1)}, s32[]{:T(128)}) while((s32[]{:T(128)}, bf16[8,20736]{1,0:T(8,128)(2,1)S(1)}, s32[16,2]{0,1:T(2,128)S(1)}, bf16[16,8,20480]{2,1,0:T(8,128)(2,1)}, s32[]{:T(128)}) %tuple.24), condition=%wide.while_cond, body=%wide.while_body.sunk | while | flops 2 | bytes 655973 | solution.py:36
  14.9 0.1 constant_dynamic-slice_fusion.2
  15.0 0.5 slice.24
  15.5 1.5 %bitcast_dynamic-update-slice_fusion.2 = bf16[16,8,20480]{2,1,0:T(8,128)(2,1)} fusion(bf16[16,8,20480]{2,1,0:T(8,128)(2,1)} %get-tuple-element.58, s32[]{:T(128)S(6)} %copy.32, bf16[8,20736]{1,0:T(8,128)(2,1)S(1)} %get-tuple-element.61, s32[]{:T(128)} %bitcast.41), kind=kLoop, calls=%fused_computation.clone.1 | loop fusion | bytes 655876 | tf_op jit(solution)/shard_map/vmap()/gather
  17.0 0.1 constant_dynamic-slice_fusion.2
  17.1 0.5 slice.24
  17.6 1.5 %bitcast_dynamic-update-slice_fusion.2 = bf16[16,8,20480]{2,1,0:T(8,128)(2,1)} fusion(bf16[16,8,20480]{2,1,0:T(8,128)(2,1)} %get-tuple-element.58, s32[]{:T(128)S(6)} %copy.32, bf16[8,20736]{1,0:T(8,128)(2,1)S(1)} %get-tuple-element.61, s32[]{:T(128)} %bitcast.41), kind=kLoop, calls=%fused_computation.clone.1 | loop fusion | bytes 655876 | tf_op jit(solution)/shard_map/vmap()/gather
  19.2 0.1 constant_dynamic-slice_fusion.2
  19.2 0.5 slice.24
  19.8 1.5 %bitcast_dynamic-update-slice_fusion.2 = bf16[16,8,20480]{2,1,0:T(8,128)(2,1)} fusion(bf16[16,8,20480]{2,1,0:T(8,128)(2,1)} %get-tuple-element.58, s32[]{:T(128)S(6)} %copy.32, bf16[8,20736]{1,0:T(8,128)(2,1)S(1)} %get-tuple-element.61, s32[]{:T(128)} %bitcast.41), kind=kLoop, calls=%fused_computation.clone.1 | loop fusion | bytes 655876 | tf_op jit(solution)/shard_map/vmap()/gather
  21.3 0.1 constant_dynamic-slice_fusion.2
  21.4 0.5 slice.24
  21.9 1.5 %bitcast_dynamic-update-slice_fusion.2 = bf16[16,8,20480]{2,1,0:T(8,128)(2,1)} fusion(bf16[16,8,20480]{2,1,0:T(8,128)(2,1)} %get-tuple-element.58, s32[]{:T(128)S(6)} %copy.32, bf16[8,20736]{1,0:T(8,128)(2,1)S(1)} %get-tuple-element.61, s32[]{:T(128)} %bitcast.41), kind=kLoop, calls=%fused_computation.clone.1 | loop fusion | bytes 655876 | tf_op jit(solution)/shard_map/vmap()/gather
  23.4 0.1 constant_dynamic-slice_fusion.2
  23.5 0.5 slice.24
  24.0 1.5 %bitcast_dynamic-update-slice_fusion.2 = bf16[16,8,20480]{2,1,0:T(8,128)(2,1)} fusion(bf16[16,8,20480]{2,1,0:T(8,128)(2,1)} %get-tuple-element.58, s32[]{:T(128)S(6)} %copy.32, bf16[8,20736]{1,0:T(8,128)(2,1)S(1)} %get-tuple-element.61, s32[]{:T(128)} %bitcast.41), kind=kLoop, calls=%fused_computation.clone.1 | loop fusion | bytes 655876 | tf_op jit(solution)/shard_map/vmap()/gather
  25.5 0.1 constant_dynamic-slice_fusion.2
  25.6 0.5 slice.24
  26.1 1.5 %bitcast_dynamic-update-slice_fusion.2 = bf16[16,8,20480]{2,1,0:T(8,128)(2,1)} fusion(bf16[16,8,20480]{2,1,0:T(8,128)(2,1)} %get-tuple-element.58, s32[]{:T(128)S(6)} %copy.32, bf16[8,20736]{1,0:T(8,128)(2,1)S(1)} %get-tuple-element.61, s32[]{:T(128)} %bitcast.41), kind=kLoop, calls=%fused_computation.clone.1 | loop fusion | bytes 655876 | tf_op jit(solution)/shard_map/vmap()/gather
  27.7 0.1 constant_dynamic-slice_fusion.2
  27.7 0.5 slice.24
  28.2 1.6 %bitcast_dynamic-update-slice_fusion.2 = bf16[16,8,20480]{2,1,0:T(8,128)(2,1)} fusion(bf16[16,8,20480]{2,1,0:T(8,128)(2,1)} %get-tuple-element.58, s32[]{:T(128)S(6)} %copy.32, bf16[8,20736]{1,0:T(8,128)(2,1)S(1)} %get-tuple-element.61, s32[]{:T(128)} %bitcast.41), kind=kLoop, calls=%fused_computation.clone.1 | loop fusion | bytes 655876 | tf_op jit(solution)/shard_map/vmap()/gather
  29.8 0.1 constant_dynamic-slice_fusion.2
  29.9 0.5 slice.24
  30.4 1.5 %bitcast_dynamic-update-slice_fusion.2 = bf16[16,8,20480]{2,1,0:T(8,128)(2,1)} fusion(bf16[16,8,20480]{2,1,0:T(8,128)(2,1)} %get-tuple-element.58, s32[]{:T(128)S(6)} %copy.32, bf16[8,20736]{1,0:T(8,128)(2,1)S(1)} %get-tuple-element.61, s32[]{:T(128)} %bitcast.41), kind=kLoop, calls=%fused_computation.clone.1 | loop fusion | bytes 655876 | tf_op jit(solution)/shard_map/vmap()/gather
  31.9 0.1 constant_dynamic-slice_fusion.2
  32.0 0.5 slice.24
  32.5 1.5 %bitcast_dynamic-update-slice_fusion.2 = bf16[16,8,20480]{2,1,0:T(8,128)(2,1)} fusion(bf16[16,8,20480]{2,1,0:T(8,128)(2,1)} %get-tuple-element.58, s32[]{:T(128)S(6)} %copy.32, bf16[8,20736]{1,0:T(8,128)(2,1)S(1)} %get-tuple-element.61, s32[]{:T(128)} %bitcast.41), kind=kLoop, calls=%fused_computation.clone.1 | loop fusion | bytes 655876 | tf_op jit(solution)/shard_map/vmap()/gather
  34.0 0.1 constant_dynamic-slice_fusion.2
  34.1 0.5 slice.24
  34.6 1.5 %bitcast_dynamic-update-slice_fusion.2 = bf16[16,8,20480]{2,1,0:T(8,128)(2,1)} fusion(bf16[16,8,20480]{2,1,0:T(8,128)(2,1)} %get-tuple-element.58, s32[]{:T(128)S(6)} %copy.32, bf16[8,20736]{1,0:T(8,128)(2,1)S(1)} %get-tuple-element.61, s32[]{:T(128)} %bitcast.41), kind=kLoop, calls=%fused_computation.clone.1 | loop fusion | bytes 655876 | tf_op jit(solution)/shard_map/vmap()/gather
  36.2 0.1 constant_dynamic-slice_fusion.2
  36.2 0.5 slice.24
  36.8 1.5 %bitcast_dynamic-update-slice_fusion.2 = bf16[16,8,20480]{2,1,0:T(8,128)(2,1)} fusion(bf16[16,8,20480]{2,1,0:T(8,128)(2,1)} %get-tuple-element.58, s32[]{:T(128)S(6)} %copy.32, bf16[8,20736]{1,0:T(8,128)(2,1)S(1)} %get-tuple-element.61, s32[]{:T(128)} %bitcast.41), kind=kLoop, calls=%fused_computation.clone.1 | loop fusion | bytes 655876 | tf_op jit(solution)/shard_map/vmap()/gather
  38.4 0.5 slice.24
  38.9 1.5 %bitcast_dynamic-update-slice_fusion.2 = bf16[16,8,20480]{2,1,0:T(8,128)(2,1)} fusion(bf16[16,8,20480]{2,1,0:T(8,128)(2,1)} %get-tuple-element.58, s32[]{:T(128)S(6)} %copy.32, bf16[8,20736]{1,0:T(8,128)(2,1)S(1)} %get-tuple-element.61, s32[]{:T(128)} %bitcast.41), kind=kLoop, calls=%fused_computation.clone.1 | loop fusion | bytes 655876 | tf_op jit(solution)/shard_map/vmap()/gather
  40.5 0.5 slice.24
  41.0 1.5 %bitcast_dynamic-update-slice_fusion.2 = bf16[16,8,20480]{2,1,0:T(8,128)(2,1)} fusion(bf16[16,8,20480]{2,1,0:T(8,128)(2,1)} %get-tuple-element.58, s32[]{:T(128)S(6)} %copy.32, bf16[8,20736]{1,0:T(8,128)(2,1)S(1)} %get-tuple-element.61, s32[]{:T(128)} %bitcast.41), kind=kLoop, calls=%fused_computation.clone.1 | loop fusion | bytes 655876 | tf_op jit(solution)/shard_map/vmap()/gather
  42.6 0.5 slice.24
  43.1 1.5 %bitcast_dynamic-update-slice_fusion.2 = bf16[16,8,20480]{2,1,0:T(8,128)(2,1)} fusion(bf16[16,8,20480]{2,1,0:T(8,128)(2,1)} %get-tuple-element.58, s32[]{:T(128)S(6)} %copy.32, bf16[8,20736]{1,0:T(8,128)(2,1)S(1)} %get-tuple-element.61, s32[]{:T(128)} %bitcast.41), kind=kLoop, calls=%fused_computation.clone.1 | loop fusion | bytes 655876 | tf_op jit(solution)/shard_map/vmap()/gather
  44.7 0.5 slice.24
  45.2 1.5 %bitcast_dynamic-update-slice_fusion.2 = bf16[16,8,20480]{2,1,0:T(8,128)(2,1)} fusion(bf16[16,8,20480]{2,1,0:T(8,128)(2,1)} %get-tuple-element.58, s32[]{:T(128)S(6)} %copy.32, bf16[8,20736]{1,0:T(8,128)(2,1)S(1)} %get-tuple-element.61, s32[]{:T(128)} %bitcast.41), kind=kLoop, calls=%fused_computation.clone.1 | loop fusion | bytes 655876 | tf_op jit(solution)/shard_map/vmap()/gather
  46.8 0.5 slice.24
  47.3 1.5 %bitcast_dynamic-update-slice_fusion.2 = bf16[16,8,20480]{2,1,0:T(8,128)(2,1)} fusion(bf16[16,8,20480]{2,1,0:T(8,128)(2,1)} %get-tuple-element.58, s32[]{:T(128)S(6)} %copy.32, bf16[8,20736]{1,0:T(8,128)(2,1)S(1)} %get-tuple-element.61, s32[]{:T(128)} %bitcast.41), kind=kLoop, calls=%fused_computation.clone.1 | loop fusion | bytes 655876 | tf_op jit(solution)/shard_map/vmap()/gather
  48.9 0.3 copy.22
  49.2 1.2 %fusion.36 = (bf16[48,159,128]{2,1,0:T(8,128)(2,1)S(1)}, bf16[48,159,128]{2,1,0:T(8,128)(2,1)S(1)}) fusion(bf16[48,160,128]{2,1,0:T(8,128)(2,1)S(1)} %bitcast.42), kind=kLoop, calls=%fused_computation.47 | loop fusion | bytes 7815168 | tf_op jit(solution)/shard_map/slice | solution.py:23
  50.4 3.1 %subtract_convert_fusion = bf16[48,160,128]{2,1,0:T(8,128)(2,1)} fusion(bf16[48,160,128]{2,1,0:T(8,128)(2,1)S(1)} %bitcast.43, bf16[48,159,128]{2,1,0:T(8,128)(2,1)S(1)} %get-tuple-element.23, bf16[48,159,128]{2,1,0:T(8,128)(2,1)S(1)} %get-tuple-element.22, s32[384]{0:T(512)S(1)} %iota_add_fusion), kind=kOutput, calls=%fused_computation.16 | convolution fusion | flops 788643840 | bytes 7841280 | tf_op jit(solution)/shard_map/rbj,ji->rbi/dot_general | solution.py:26
  53.5 3.7 %dot_general.9 = bf16[8,6,20480]{2,1,0:T(8,128)(2,1)S(1)} reshape(bf16[48,160,128]{2,1,0:T(8,128)(2,1)} %subtract_convert_fusion) | data formatting | bytes 3932160 | tf_op jit(solution)/shard_map/mb,sb->ms/dot_general | solution.py:53
  57.3 13.3 %fusion.12 = f32[8,16,8,6]{2,0,3,1:T(8,128)S(1)} fusion(bf16[16,8,20480]{2,1,0:T(8,128)(2,1)} %get-tuple-element.9, bf16[8,6,20480]{2,1,0:T(8,128)(2,1)S(1)} %dot_general.9), kind=kOutput, calls=%fused_computation.14 | convolution fusion | flops 251658240 | bytes 7233536 | tf_op jit(solution)/shard_map/mb,sb->ms/dot_general | solution.py:53
  70.6 0.2 copy.19
  70.8 0.7 reshape.74
  71.6 4.9 %all-to-all-start = ((f32[8,1,768]{2,1,0:T(1,128)}), f32[8,1,768]{2,1,0:T(1,128)S(1)}, u32[]{:S(2)}, u32[]{:S(2)}) async-start(f32[8,1,768]{2,1,0:T(1,128)} %reshape.74), calls=%async_computation | async-start | bytes 49152 | tf_op jit(solution)/shard_map/all_to_all | solution.py:58
  76.5 0.1 dynamic-slice_add_fusion
  76.6 0.1 compare_and_fusion
  76.6 5.5 %all-to-all-done = f32[8,1,768]{2,1,0:T(1,128)S(1)} async-done(((f32[8,1,768]{2,1,0:T(1,128)}), f32[8,1,768]{2,1,0:T(1,128)S(1)}, u32[]{:S(2)}, u32[]{:S(2)}) %all-to-all-start) | async-done | bytes 24608 | tf_op jit(solution)/shard_map/all_to_all | solution.py:58
  82.2 0.5 broadcast.91
  82.7 0.7 reduce.2
  83.4 0.1 reshape.75
  83.5 0.7 fusion.20
  84.2 0.7 divide_bitcast_fusion
  (16 shorter events, 0.4 us)
Async XLA Ops:
  0.6 48.3 %copy-start = (bf16[48,20480]{1,0:T(8,128)(2,1)S(1)}, bf16[48,20480]{1,0:T(8,128)(2,1)}, u32[]{:S(2)}) copy-start(bf16[48,20480]{1,0:T(8,128)(2,1)} %param.5) | copy-start | bytes 5898244
  57.2 19.2 %copy-start.1 = (s32[48]{0:T(128)S(1)}, s32[48]{0:T(128)}, u32[]{:S(2)}) copy-start(s32[48]{0:T(128)} %param.9) | copy-start | bytes 580
  57.3 19.2 %copy-start.2 = (s32[48]{0:T(128)S(1)}, s32[48]{0:T(128)}, u32[]{:S(2)}) copy-start(s32[48]{0:T(128)} %param.8) | copy-start | bytes 580
  71.6 10.6 %all-to-all-start = ((f32[8,1,768]{2,1,0:T(1,128)}), f32[8,1,768]{2,1,0:T(1,128)S(1)}, u32[]{:S(2)}, u32[]{:S(2)}) async-start(f32[8,1,768]{2,1,0:T(1,128)} %reshape.74), calls=%async_computation | async-start | bytes 49152 | tf_op jit(solution)/shard_map/all_to_all | solution.py:58
where the time goes:
time: 85.3 us; the launch traced here: 84.9 us
  local copies, waits for them, and re-layouts  42.3 us (50%)
  matrix products  16.4 us (19%)
  blocking collectives  12 us (14%)
  waiting for transfers between devices  5.51 us (6%)
  starting transfers between devices  4.88 us (6%)
  other arithmetic  2.93 us (3%)
    gather x48, local copies, waits for them, and re-layouts  33.9 us
    dot_general x1, matrix products, local(): jnp.einsum('mb,sb->ms', copies, corrected, preferred_element_type=jnp.flo...  13.3 us
    all_gather x1, blocking collectives, local(): piece = lax.all_gather(theo, 'band', axis=1, tiled=True)  12 us
    all_to_all x1, waiting for transfers between devices, local(): lax.all_to_all(score_table, 'query', split_axis=2, concat_axis=0, tiled=T...  5.51 us
    all_to_all x1, starting transfers between devices, local(): lax.all_to_all(score_table, 'query', split_axis=2, concat_axis=0, tiled=T...  4.88 us
    dot_general x2, local copies, waits for them, and re-layouts, local(): jnp.einsum('mb,sb->ms', copies, corrected, preferred_element_type=jnp.flo...  3.95 us
    dot_general x1, matrix products, correct(): jnp.einsum('rbj,ji->rbi', stacked, box_table(), preferred_element_type=jn...  3.08 us
    unnamed x11, local copies, waits for them, and re-layouts  2.71 us
  transfers between devices with their start and end apart: 1, of which 1 were waited for; matrix products, arithmetic and copies ran while one was open for 0% of the time, Pallas kernels for 0%

commit v1 on v0

--- a/solution.py
+++ b/solution.py
@@ -55,7 +55,15 @@
     score_table = scores.reshape(group_size, shift_count, query_count, own_rows)
     low_own = lax.dynamic_slice_in_dim(win_lo, own_start, own_rows, 0)
     length_own = lax.dynamic_slice_in_dim(win_len, own_start, own_rows, 0)
-    gathered = lax.all_to_all(score_table, "query", split_axis=2, concat_axis=0, tiled=True)
+    ways, here = (lax.axis_size("query"), lax.axis_index("query"))
+    width = score_table.shape[2] // ways
+    turned = jnp.roll(score_table, -here * width, axis=2)
+    got = [lax.slice_in_dim(turned, 0, width, axis=2)]
+    for far in range(1, ways):
+        sent = lax.slice_in_dim(turned, far * width, (far + 1) * width, axis=2)
+        got.append(lax.ppermute(sent, "query", [(d, (d + far) % ways) for d in range(ways)]))
+    line = jnp.concatenate(got[::-1], axis=0)
+    gathered = jnp.roll(line, (here + 1) * got[0].shape[0], axis=0)
     total_peptides = gathered.shape[0]
     owned_scores = gathered.reshape(total_peptides, shift_count, own_rows)
     peptide_index = lax.broadcasted_iota(jnp.int32, (total_peptides, own_rows), 0)

time: 85.3 us -> 150 us (1.76)
  waiting for transfers between devices: 5.51 us -> 56.9 us
  local copies, waits for them, and re-layouts: 42.3 us -> 51.8 us
  starting transfers between devices: 4.88 us -> 9.12 us
    ppermute x0 -> x7, waiting for transfers between devices: none -> 56.9 us  [local(): lax.ppermute(sent, 'query', [(d, (d + far) % ways) for d in range(ways)])]
    ppermute x0 -> x7, local copies, waits for them, and re-layouts: none -> 9.38 us  [local(): lax.ppermute(sent, 'query', [(d, (d + far) % ways) for d in range(ways)])]
    ppermute x0 -> x7, starting transfers between devices: none -> 9.12 us  [local(): lax.ppermute(sent, 'query', [(d, (d + far) % ways) for d in range(ways)])]
    all_to_all x1 -> x0, waiting for transfers between devices: 5.51 us -> none  [local(): lax.all_to_all(score_table, 'query', split_axis=2, concat_axis=0, tiled=T...]
    all_to_all x1 -> x0, starting transfers between devices: 4.88 us -> none  [local(): lax.all_to_all(score_table, 'query', split_axis=2, concat_axis=0, tiled=T...]
    dot_general x2 -> x1, local copies, waits for them, and re-layouts: 3.95 us -> 3.71 us  [local(): jnp.einsum('mb,sb->ms', copies, corrected, preferred_element_type=jnp.flo...]
  transfers between devices with their start and end apart: 1 -> 7, of which waited for: 1 -> 4; matrix products, arithmetic and copies ran while one was open for 0% -> 6% of each run, Pallas kernels for 0% -> 0%
where the time goes in v1:
time: 150 us
  waiting for transfers between devices  56.9 us (38%)
  local copies, waits for them, and re-layouts  51.8 us (35%)
  matrix products  16.4 us (11%)
  blocking collectives  12 us (8%)
  starting transfers between devices  9.12 us (6%)
  other arithmetic  2.53 us (2%)
    ppermute x7, waiting for transfers between devices, local(): lax.ppermute(sent, 'query', [(d, (d + far) % ways) for d in range(ways)])  56.9 us
    gather x48, local copies, waits for them, and re-layouts  33.9 us
    dot_general x1, matrix products, local(): jnp.einsum('mb,sb->ms', copies, corrected, preferred_element_type=jnp.flo...  13.3 us
    all_gather x1, blocking collectives, local(): piece = lax.all_gather(theo, 'band', axis=1, tiled=True)  12 us
    ppermute x7, local copies, waits for them, and re-layouts, local(): lax.ppermute(sent, 'query', [(d, (d + far) % ways) for d in range(ways)])  9.38 us
    ppermute x7, starting transfers between devices, local(): lax.ppermute(sent, 'query', [(d, (d + far) % ways) for d in range(ways)])  9.12 us
    dot_general x1, local copies, waits for them, and re-layouts, local(): jnp.einsum('mb,sb->ms', copies, corrected, preferred_element_type=jnp.flo...  3.71 us
    dot_general x1, matrix products, correct(): jnp.einsum('rbj,ji->rbi', stacked, box_table(), preferred_element_type=jn...  3.09 us
  transfers between devices with their start and end apart: 7, of which 4 were waited for; matrix products, arithmetic and copies ran while one was open for 6% of the time, Pallas kernels for 0%

profile of v1, /device:TPU:0, one launch (start us, length us, event | category | flops | bytes accessed | tf_op | source)
XLA Modules:
  0.0 149.6 jit_solution(16308068733184761514)
XLA Ops:
  0.7 1.1 copy.30
  1.8 12.0 %all_gather.3 = bf16[1,8,20480]{2,0,1:T(2,128)(2,1)S(1)} all-gather(bf16[1,2,20480]{2,0,1:T(2,128)(2,1)S(1)} %copy.30), channel_id=1, replica_groups=mesh['band'=4,'query'=8] {'band'}, dimensions={1}, use_global_device_ids=true | all-gather | bytes 409600 | tf_op jit(solution)/shard_map/all_gather | solution.py:50
  13.9 0.4 copy.56
  14.2 0.7 fusion.31
  14.9 34.0 %while.1 = (s32[]{:T(128)}, bf16[8,20736]{1,0:T(8,128)(2,1)S(1)}, s32[16,2]{0,1:T(2,128)S(1)}, bf16[16,8,20480]{2,1,0:T(8,128)(2,1)}, s32[]{:T(128)}) while((s32[]{:T(128)}, bf16[8,20736]{1,0:T(8,128)(2,1)S(1)}, s32[16,2]{0,1:T(2,128)S(1)}, bf16[16,8,20480]{2,1,0:T(8,128)(2,1)}, s32[]{:T(128)}) %tuple.31), condition=%wide.while_cond, body=%wide.while_body.sunk | while | flops 2 | bytes 655973 | solution.py:36
  15.0 0.5 slice.72
  15.5 1.5 %bitcast_dynamic-update-slice_fusion.2 = bf16[16,8,20480]{2,1,0:T(8,128)(2,1)} fusion(bf16[16,8,20480]{2,1,0:T(8,128)(2,1)} %get-tuple-element.66, s32[]{:T(128)S(6)} %copy.60, bf16[8,20736]{1,0:T(8,128)(2,1)S(1)} %get-tuple-element.69, s32[]{:T(128)} %bitcast.36), kind=kLoop, calls=%fused_computation.clone.1 | loop fusion | bytes 655876 | tf_op jit(solution)/shard_map/vmap()/gather
  17.1 0.5 slice.72
  17.7 1.5 %bitcast_dynamic-update-slice_fusion.2 = bf16[16,8,20480]{2,1,0:T(8,128)(2,1)} fusion(bf16[16,8,20480]{2,1,0:T(8,128)(2,1)} %get-tuple-element.66, s32[]{:T(128)S(6)} %copy.60, bf16[8,20736]{1,0:T(8,128)(2,1)S(1)} %get-tuple-element.69, s32[]{:T(128)} %bitcast.36), kind=kLoop, calls=%fused_computation.clone.1 | loop fusion | bytes 655876 | tf_op jit(solution)/shard_map/vmap()/gather
  19.3 0.5 slice.72
  19.8 1.5 %bitcast_dynamic-update-slice_fusion.2 = bf16[16,8,20480]{2,1,0:T(8,128)(2,1)} fusion(bf16[16,8,20480]{2,1,0:T(8,128)(2,1)} %get-tuple-element.66, s32[]{:T(128)S(6)} %copy.60, bf16[8,20736]{1,0:T(8,128)(2,1)S(1)} %get-tuple-element.69, s32[]{:T(128)} %bitcast.36), kind=kLoop, calls=%fused_computation.clone.1 | loop fusion | bytes 655876 | tf_op jit(solution)/shard_map/vmap()/gather
  21.4 0.5 slice.72
  21.9 1.5 %bitcast_dynamic-update-slice_fusion.2 = bf16[16,8,20480]{2,1,0:T(8,128)(2,1)} fusion(bf16[16,8,20480]{2,1,0:T(8,128)(2,1)} %get-tuple-element.66, s32[]{:T(128)S(6)} %copy.60, bf16[8,20736]{1,0:T(8,128)(2,1)S(1)} %get-tuple-element.69, s32[]{:T(128)} %bitcast.36), kind=kLoop, calls=%fused_computation.clone.1 | loop fusion | bytes 655876 | tf_op jit(solution)/shard_map/vmap()/gather
  23.5 0.5 slice.72
  24.0 1.5 %bitcast_dynamic-update-slice_fusion.2 = bf16[16,8,20480]{2,1,0:T(8,128)(2,1)} fusion(bf16[16,8,20480]{2,1,0:T(8,128)(2,1)} %get-tuple-element.66, s32[]{:T(128)S(6)} %copy.60, bf16[8,20736]{1,0:T(8,128)(2,1)S(1)} %get-tuple-element.69, s32[]{:T(128)} %bitcast.36), kind=kLoop, calls=%fused_computation.clone.1 | loop fusion | bytes 655876 | tf_op jit(solution)/shard_map/vmap()/gather
  25.6 0.5 slice.72
  26.1 1.5 %bitcast_dynamic-update-slice_fusion.2 = bf16[16,8,20480]{2,1,0:T(8,128)(2,1)} fusion(bf16[16,8,20480]{2,1,0:T(8,128)(2,1)} %get-tuple-element.66, s32[]{:T(128)S(6)} %copy.60, bf16[8,20736]{1,0:T(8,128)(2,1)S(1)} %get-tuple-element.69, s32[]{:T(128)} %bitcast.36), kind=kLoop, calls=%fused_computation.clone.1 | loop fusion | bytes 655876 | tf_op jit(solution)/shard_map/vmap()/gather
  27.7 0.5 slice.72
  28.2 1.6 %bitcast_dynamic-update-slice_fusion.2 = bf16[16,8,20480]{2,1,0:T(8,128)(2,1)} fusion(bf16[16,8,20480]{2,1,0:T(8,128)(2,1)} %get-tuple-element.66, s32[]{:T(128)S(6)} %copy.60, bf16[8,20736]{1,0:T(8,128)(2,1)S(1)} %get-tuple-element.69, s32[]{:T(128)} %bitcast.36), kind=kLoop, calls=%fused_computation.clone.1 | loop fusion | bytes 655876 | tf_op jit(solution)/shard_map/vmap()/gather
  29.9 0.5 slice.72
  30.4 1.5 %bitcast_dynamic-update-slice_fusion.2 = bf16[16,8,20480]{2,1,0:T(8,128)(2,1)} fusion(bf16[16,8,20480]{2,1,0:T(8,128)(2,1)} %get-tuple-element.66, s32[]{:T(128)S(6)} %copy.60, bf16[8,20736]{1,0:T(8,128)(2,1)S(1)} %get-tuple-element.69, s32[]{:T(128)} %bitcast.36), kind=kLoop, calls=%fused_computation.clone.1 | loop fusion | bytes 655876 | tf_op jit(solution)/shard_map/vmap()/gather
  32.0 0.5 slice.72
  32.5 1.5 %bitcast_dynamic-update-slice_fusion.2 = bf16[16,8,20480]{2,1,0:T(8,128)(2,1)} fusion(bf16[16,8,20480]{2,1,0:T(8,128)(2,1)} %get-tuple-element.66, s32[]{:T(128)S(6)} %copy.60, bf16[8,20736]{1,0:T(8,128)(2,1)S(1)} %get-tuple-element.69, s32[]{:T(128)} %bitcast.36), kind=kLoop, calls=%fused_computation.clone.1 | loop fusion | bytes 655876 | tf_op jit(solution)/shard_map/vmap()/gather
  34.1 0.5 slice.72
  34.6 1.5 %bitcast_dynamic-update-slice_fusion.2 = bf16[16,8,20480]{2,1,0:T(8,128)(2,1)} fusion(bf16[16,8,20480]{2,1,0:T(8,128)(2,1)} %get-tuple-element.66, s32[]{:T(128)S(6)} %copy.60, bf16[8,20736]{1,0:T(8,128)(2,1)S(1)} %get-tuple-element.69, s32[]{:T(128)} %bitcast.36), kind=kLoop, calls=%fused_computation.clone.1 | loop fusion | bytes 655876 | tf_op jit(solution)/shard_map/vmap()/gather
  36.3 0.5 slice.72
  36.8 1.5 %bitcast_dynamic-update-slice_fusion.2 = bf16[16,8,20480]{2,1,0:T(8,128)(2,1)} fusion(bf16[16,8,20480]{2,1,0:T(8,128)(2,1)} %get-tuple-element.66, s32[]{:T(128)S(6)} %copy.60, bf16[8,20736]{1,0:T(8,128)(2,1)S(1)} %get-tuple-element.69, s32[]{:T(128)} %bitcast.36), kind=kLoop, calls=%fused_computation.clone.1 | loop fusion | bytes 655876 | tf_op jit(solution)/shard_map/vmap()/gather
  38.4 0.5 slice.72
  38.9 1.5 %bitcast_dynamic-update-slice_fusion.2 = bf16[16,8,20480]{2,1,0:T(8,128)(2,1)} fusion(bf16[16,8,20480]{2,1,0:T(8,128)(2,1)} %get-tuple-element.66, s32[]{:T(128)S(6)} %copy.60, bf16[8,20736]{1,0:T(8,128)(2,1)S(1)} %get-tuple-element.69, s32[]{:T(128)} %bitcast.36), kind=kLoop, calls=%fused_computation.clone.1 | loop fusion | bytes 655876 | tf_op jit(solution)/shard_map/vmap()/gather
  40.5 0.5 slice.72
  41.0 1.5 %bitcast_dynamic-update-slice_fusion.2 = bf16[16,8,20480]{2,1,0:T(8,128)(2,1)} fusion(bf16[16,8,20480]{2,1,0:T(8,128)(2,1)} %get-tuple-element.66, s32[]{:T(128)S(6)} %copy.60, bf16[8,20736]{1,0:T(8,128)(2,1)S(1)} %get-tuple-element.69, s32[]{:T(128)} %bitcast.36), kind=kLoop, calls=%fused_computation.clone.1 | loop fusion | bytes 655876 | tf_op jit(solution)/shard_map/vmap()/gather
  42.6 0.5 slice.72
  43.1 1.5 %bitcast_dynamic-update-slice_fusion.2 = bf16[16,8,20480]{2,1,0:T(8,128)(2,1)} fusion(bf16[16,8,20480]{2,1,0:T(8,128)(2,1)} %get-tuple-element.66, s32[]{:T(128)S(6)} %copy.60, bf16[8,20736]{1,0:T(8,128)(2,1)S(1)} %get-tuple-element.69, s32[]{:T(128)} %bitcast.36), kind=kLoop, calls=%fused_computation.clone.1 | loop fusion | bytes 655876 | tf_op jit(solution)/shard_map/vmap()/gather
  44.7 0.5 slice.72
  45.2 1.5 %bitcast_dynamic-update-slice_fusion.2 = bf16[16,8,20480]{2,1,0:T(8,128)(2,1)} fusion(bf16[16,8,20480]{2,1,0:T(8,128)(2,1)} %get-tuple-element.66, s32[]{:T(128)S(6)} %copy.60, bf16[8,20736]{1,0:T(8,128)(2,1)S(1)} %get-tuple-element.69, s32[]{:T(128)} %bitcast.36), kind=kLoop, calls=%fused_computation.clone.1 | loop fusion | bytes 655876 | tf_op jit(solution)/shard_map/vmap()/gather
  46.9 0.5 slice.72
  47.4 1.5 %bitcast_dynamic-update-slice_fusion.2 = bf16[16,8,20480]{2,1,0:T(8,128)(2,1)} fusion(bf16[16,8,20480]{2,1,0:T(8,128)(2,1)} %get-tuple-element.66, s32[]{:T(128)S(6)} %copy.60, bf16[8,20736]{1,0:T(8,128)(2,1)S(1)} %get-tuple-element.69, s32[]{:T(128)} %bitcast.36), kind=kLoop, calls=%fused_computation.clone.1 | loop fusion | bytes 655876 | tf_op jit(solution)/shard_map/vmap()/gather
  48.9 0.3 copy.50
  49.2 1.2 fusion.37
  50.4 3.1 %subtract_convert_fusion = bf16[48,160,128]{2,1,0:T(8,128)(2,1)} fusion(bf16[48,160,128]{2,1,0:T(8,128)(2,1)S(1)} %bitcast.38, bf16[48,159,128]{2,1,0:T(8,128)(2,1)S(1)} %get-tuple-element.23, bf16[48,159,128]{2,1,0:T(8,128)(2,1)S(1)} %get-tuple-element.22, s32[384]{0:T(512)S(1)} %iota_add_fusion), kind=kOutput, calls=%fused_computation.16 | convolution fusion | flops 788643840 | bytes 7841280 | tf_op jit(solution)/shard_map/rbj,ji->rbi/dot_general | solution.py:26
  53.5 3.7 %dot_general.9 = bf16[8,6,20480]{2,1,0:T(8,128)(2,1)S(1)} reshape(bf16[48,160,128]{2,1,0:T(8,128)(2,1)} %subtract_convert_fusion) | data formatting | bytes 3932160 | tf_op jit(solution)/shard_map/mb,sb->ms/dot_general | solution.py:53
  57.3 13.3 %fusion.12 = f32[8,16,8,6]{2,0,3,1:T(8,128)S(1)} fusion(bf16[16,8,20480]{2,1,0:T(8,128)(2,1)} %get-tuple-element.9, bf16[8,6,20480]{2,1,0:T(8,128)(2,1)S(1)} %dot_general.9), kind=kOutput, calls=%fused_computation.14 | convolution fusion | flops 251658240 | bytes 7233536 | tf_op jit(solution)/shard_map/mb,sb->ms/dot_general | solution.py:53
  70.6 0.3 dynamic-slice_maximum_fusion
  70.9 0.8 fusion.38
  71.7 1.1 collective-permute-start
  72.8 2.6 %collective-permute-start.1 = (f32[8,16,1,6]{2,0,3,1:T(8,128)S(1)}, f32[8,16,1,6]{2,0,3,1:T(8,128)}, u32[]{:S(2)}, u32[]{:S(2)}) collective-permute-start(f32[8,16,1,6]{2,0,3,1:T(8,128)S(1)} %get-tuple-element.30), channel_id=1, source_target_pairs={{0,6},{1,7},{2,0},{3,1},{4,2},{5,3},{6,4},{7,5},{8,14},{9,15},{10,... | collective-permute-start | bytes 9224 | tf_op jit(solution)/shard_map/ppermute | solution.py:64
  75.4 2.7 %collective-permute-start.3 = (f32[8,16,1,6]{2,0,3,1:T(8,128)S(1)}, f32[8,16,1,6]{2,0,3,1:T(8,128)}, u32[]{:S(2)}, u32[]{:S(2)}) collective-permute-start(f32[8,16,1,6]{2,0,3,1:T(8,128)S(1)} %get-tuple-element.28), channel_id=1, source_target_pairs={{0,4},{1,5},{2,6},{3,7},{4,0},{5,1},{6,2},{7,3},{8,12},{9,13},{10,... | collective-permute-start | bytes 9224 | tf_op jit(solution)/shard_map/ppermute | solution.py:64
  78.1 0.1 dynamic-slice_add_fusion
  78.2 1.9 %collective-permute-done = f32[8,16,1,6]{2,0,3,1:T(8,128)} collective-permute-done((f32[8,16,1,6]{2,0,3,1:T(8,128)S(1)}, f32[8,16,1,6]{2,0,3,1:T(8,128)}, u32[]{:S(2)}, u32[]{:S(2)}) %collective-permute-start) | collective-permute-done | bytes 3104 | tf_op jit(solution)/shard_map/ppermute | solution.py:64
  80.1 2.7 %collective-permute-start.5 = (f32[8,16,1,6]{2,0,3,1:T(8,128)S(1)}, f32[8,16,1,6]{2,0,3,1:T(8,128)S(1)}, u32[]{:S(2)}, u32[]{:S(2)}) collective-permute-start(f32[8,16,1,6]{2,0,3,1:T(8,128)S(1)} %get-tuple-element.26), channel_id=1, source_target_pairs={{0,2},{1,3},{2,4},{3,5},{4,6},{5,7},{6,0},{7,1},{8,10},{9,11},{10,... | collective-permute-start | bytes 9224 | tf_op jit(solution)/shard_map/ppermute | solution.py:64
  82.8 9.0 %collective-permute-done.1 = f32[8,16,1,6]{2,0,3,1:T(8,128)} collective-permute-done((f32[8,16,1,6]{2,0,3,1:T(8,128)S(1)}, f32[8,16,1,6]{2,0,3,1:T(8,128)}, u32[]{:S(2)}, u32[]{:S(2)}) %collective-permute-start.1) | collective-permute-done | bytes 3104 | tf_op jit(solution)/shard_map/ppermute | solution.py:64
  91.9 0.6 copy.39
  92.5 1.6 %copy.32 = f32[8,16,1,6]{0,1,3,2:T(8,128)S(1)} copy(f32[8,16,1,6]{2,0,3,1:T(8,128)} %collective-permute-done) | data formatting | bytes 6144 | tf_op jit(solution)/shard_map/ppermute | solution.py:64
  94.1 1.6 %copy.33 = f32[8,16,1,6]{0,1,3,2:T(8,128)S(1)} copy(f32[8,16,1,6]{2,0,3,1:T(8,128)} %collective-permute-done.1) | data formatting | bytes 6144 | tf_op jit(solution)/shard_map/ppermute | solution.py:64
  95.7 1.3 collective-permute-done.2
  97.0 1.6 %copy.34 = f32[8,16,1,6]{0,1,3,2:T(8,128)S(1)} copy(f32[8,16,1,6]{2,0,3,1:T(8,128)} %collective-permute-done.2) | data formatting | bytes 6144 | tf_op jit(solution)/shard_map/ppermute | solution.py:64
  98.6 44.7 %collective-permute-done.3 = f32[8,16,1,6]{2,0,3,1:T(8,128)} collective-permute-done((f32[8,16,1,6]{2,0,3,1:T(8,128)S(1)}, f32[8,16,1,6]{2,0,3,1:T(8,128)}, u32[]{:S(2)}, u32[]{:S(2)}) %collective-permute-start.3) | collective-permute-done | bytes 3104 | tf_op jit(solution)/shard_map/ppermute | solution.py:64
  143.4 1.6 %copy.35 = f32[8,16,1,6]{0,1,3,2:T(8,128)S(1)} copy(f32[8,16,1,6]{2,0,3,1:T(8,128)} %collective-permute-done.3) | data formatting | bytes 6144 | tf_op jit(solution)/shard_map/ppermute | solution.py:64
  145.0 1.6 %copy.36 = f32[8,16,1,6]{0,1,3,2:T(8,128)S(1)} copy(f32[8,16,1,6]{2,0,3,1:T(8,128)} %collective-permute-done.4) | data formatting | bytes 6144 | tf_op jit(solution)/shard_map/ppermute | solution.py:64
  146.6 0.6 copy.37
  147.2 0.6 copy.38
  147.9 0.3 concatenate.27
  148.2 0.8 fusion.28
  148.9 0.7 divide_bitcast_fusion
  (33 shorter events, 1.3 us)
Async XLA Ops:
  0.6 48.3 %copy-start = (bf16[48,20480]{1,0:T(8,128)(2,1)S(1)}, bf16[48,20480]{1,0:T(8,128)(2,1)}, u32[]{:S(2)}) copy-start(bf16[48,20480]{1,0:T(8,128)(2,1)} %param.5) | copy-start | bytes 5898244
  70.6 7.5 %copy-start.1 = (s32[48]{0:T(128)S(1)}, s32[48]{0:T(128)}, u32[]{:S(2)}) copy-start(s32[48]{0:T(128)} %param.9) | copy-start | bytes 580
  70.6 7.5 %copy-start.2 = (s32[48]{0:T(128)S(1)}, s32[48]{0:T(128)}, u32[]{:S(2)}) copy-start(s32[48]{0:T(128)} %param.8) | copy-start | bytes 580
  71.7 8.4 %collective-permute-start = (f32[8,16,1,6]{2,0,3,1:T(8,128)S(1)}, f32[8,16,1,6]{2,0,3,1:T(8,128)}, u32[]{:S(2)}, u32[]{:S(2)}) collective-permute-start(f32[8,16,1,6]{2,0,3,1:T(8,128)S(1)} %get-tuple-element.31), channel_id=1, source_target_pairs={{0,7},{1,0},{2,1},{3,2},{4,3},{5,4},{6,5},{7,6},{8,15},{9,8},{10,9... | collective-permute-start | bytes 9224 | tf_op jit(solution)/shard_map/ppermute | solution.py:64
  72.8 19.0 %collective-permute-start.1 = (f32[8,16,1,6]{2,0,3,1:T(8,128)S(1)}, f32[8,16,1,6]{2,0,3,1:T(8,128)}, u32[]{:S(2)}, u32[]{:S(2)}) collective-permute-start(f32[8,16,1,6]{2,0,3,1:T(8,128)S(1)} %get-tuple-element.30), channel_id=1, source_target_pairs={{0,6},{1,7},{2,0},{3,1},{4,2},{5,3},{6,4},{7,5},{8,14},{9,15},{10,... | collective-permute-start | bytes 9224 | tf_op jit(solution)/shard_map/ppermute | solution.py:64
  75.4 21.6 %collective-permute-start.2 = (f32[8,16,1,6]{2,0,3,1:T(8,128)S(1)}, f32[8,16,1,6]{2,0,3,1:T(8,128)}, u32[]{:S(2)}, u32[]{:S(2)}) collective-permute-start(f32[8,16,1,6]{2,0,3,1:T(8,128)S(1)} %get-tuple-element.29), channel_id=1, source_target_pairs={{0,5},{1,6},{2,7},{3,0},{4,1},{5,2},{6,3},{7,4},{8,13},{9,14},{10,... | collective-permute-start | bytes 9224 | tf_op jit(solution)/shard_map/ppermute | solution.py:64
  75.4 68.0 %collective-permute-start.3 = (f32[8,16,1,6]{2,0,3,1:T(8,128)S(1)}, f32[8,16,1,6]{2,0,3,1:T(8,128)}, u32[]{:S(2)}, u32[]{:S(2)}) collective-permute-start(f32[8,16,1,6]{2,0,3,1:T(8,128)S(1)} %get-tuple-element.28), channel_id=1, source_target_pairs={{0,4},{1,5},{2,6},{3,7},{4,0},{5,1},{6,2},{7,3},{8,12},{9,13},{10,... | collective-permute-start | bytes 9224 | tf_op jit(solution)/shard_map/ppermute | solution.py:64
  78.1 66.9 %collective-permute-start.4 = (f32[8,16,1,6]{2,0,3,1:T(8,128)S(1)}, f32[8,16,1,6]{2,0,3,1:T(8,128)}, u32[]{:S(2)}, u32[]{:S(2)}) collective-permute-start(f32[8,16,1,6]{2,0,3,1:T(8,128)S(1)} %get-tuple-element.27), channel_id=1, source_target_pairs={{0,3},{1,4},{2,5},{3,6},{4,7},{5,0},{6,1},{7,2},{8,11},{9,12},{10,... | collective-permute-start | bytes 9224 | tf_op jit(solution)/shard_map/ppermute | solution.py:64
  80.1 66.5 %collective-permute-start.5 = (f32[8,16,1,6]{2,0,3,1:T(8,128)S(1)}, f32[8,16,1,6]{2,0,3,1:T(8,128)S(1)}, u32[]{:S(2)}, u32[]{:S(2)}) collective-permute-start(f32[8,16,1,6]{2,0,3,1:T(8,128)S(1)} %get-tuple-element.26), channel_id=1, source_target_pairs={{0,2},{1,3},{2,4},{3,5},{4,6},{5,7},{6,0},{7,1},{8,10},{9,11},{10,... | collective-permute-start | bytes 9224 | tf_op jit(solution)/shard_map/ppermute | solution.py:64
  91.8 55.5 %collective-permute-start.6 = (f32[8,16,1,6]{2,0,3,1:T(8,128)S(1)}, f32[8,16,1,6]{2,0,3,1:T(8,128)S(1)}, u32[]{:S(2)}, u32[]{:S(2)}) collective-permute-start(f32[8,16,1,6]{2,0,3,1:T(8,128)S(1)} %get-tuple-element.25), channel_id=1, source_target_pairs={{0,1},{1,2},{2,3},{3,4},{4,5},{5,6},{6,7},{7,0},{8,9},{9,10},{10,1... | collective-permute-start | bytes 9224 | tf_op jit(solution)/shard_map/ppermute | solution.py:64
